TPU v7x, 256 devices: a whole 4x4x8 slice. The times are simulated.
256 devices in a mesh: chan: 16 (over z, core), rad: 16 (over y, x).
Axes of the slice: x: 4, y: 4, z: 8, core: 2. Of those that a mesh axis runs over, the one named last changes fastest.
Arguments:
- state: float32 [2048, 2, 16, 1536], P('chan', None, None, 'rad'), may hold values from -200 to 200
- coupling: float32 [64, 16, 4, 32, 32], P('chan'), may hold values from -1.1 to 1.1
- fetch_group: int32 [16, 16], replicated, may hold values from 0 to 3
- live_slots: int32 [64], P('chan'), may hold values from 1 to 16, as said below
- radius_one: float32 [16], replicated, may hold values from 1 to 6
- radius_two: float32 [1536], P('rad'), may hold values from 1 to 6
- kinetic_diag: float32 [12, 128, 128], replicated, may hold values from -2 to 5
- kinetic_link: float32 [11, 128, 128], replicated, may hold values from -0.5 to 0.5
Outputs:
- orthogonal: float32 [2048, 2, 16, 1536], P(('chan', 'rad'))
- arnoldi_coeffs: float32 [3], replicated
Inputs may be any that keep to these rules, and one draw needn't show every extreme that they name: `live_slots`: every draw has a block with all 16 slots live.
All inputs are finite; a program needn't handle non-finite values.
Results may differ from a plain program's by a relative error of at most 0.0003.
Values sent between devices are 32-bit elements; how exact they have to be, the bound alone decides.
A program may use at most 128 MiB of HBM per device.

v0:
```python
import jax
import jax.numpy as jnp
from jax import lax
from jax.sharding import PartitionSpec as P

C = 2048
R = 1536


def radial_kernel(radius_one, radius_two, orders):
    nearer = jnp.minimum(radius_one[:, None], radius_two[None, :])
    farther = jnp.maximum(radius_one[:, None], radius_two[None, :])
    powers = jnp.arange(orders).astype(radius_one.dtype)[:, None, None]
    return nearer[None] ** powers / farther[None] ** (powers + 1.0)


def kinetic(field, kinetic_diag, kinetic_link):
    elements = kinetic_diag.shape[0]
    points = kinetic_diag.shape[1]
    rows = field.reshape(-1, elements, points)
    result = jnp.einsum("rep,eqp->req", rows, kinetic_diag, precision=lax.Precision.HIGHEST)
    lower = jnp.einsum("rep,eqp->req", rows[:, :-1], kinetic_link, precision=lax.Precision.HIGHEST)
    upper = jnp.einsum("rep,epq->req", rows[:, 1:], kinetic_link, precision=lax.Precision.HIGHEST)
    result = (
        result + jnp.pad(lower, ((0, 0), (1, 0), (0, 0))) + jnp.pad(upper, ((0, 0), (0, 1), (0, 0)))
    )
    return result.reshape(field.shape)


def coupling_products(state, coupling, fetch_group, live_slots, radius_one, radius_two):
    chan_count = lax.axis_size("chan")
    my_rank = lax.axis_index("chan")
    local_channels = state.shape[0]
    planes = state.shape[1]
    band = state.shape[2]
    radial = state.shape[3]
    groups_here = coupling.shape[0]
    orders = coupling.shape[2]
    block = coupling.shape[3]
    cells = planes * band * radial
    grouped = state.reshape(groups_here, block, cells)
    outgoing = jnp.take(grouped, fetch_group[:, my_rank], axis=0)
    incoming = lax.all_to_all(outgoing, "chan", split_axis=0, concat_axis=0, tiled=True)
    incoming = incoming.reshape(chan_count * block, cells)
    slot_of = (jnp.arange(chan_count, dtype=jnp.int32) - my_rank) % chan_count
    weights = jnp.take(coupling, slot_of, axis=1)
    active = (slot_of[None, :] < live_slots[:, None]).astype(jnp.float32)
    weights = weights * active[:, :, None, None, None]
    matrices = weights.transpose(2, 0, 3, 1, 4).reshape(orders, local_channels, chan_count * block)
    kernel = radial_kernel(radius_one, radius_two, orders)
    kernel = jnp.broadcast_to(kernel[:, None], (orders, planes, band, radial)).reshape(
        orders, cells
    )
    total = jnp.zeros((local_channels, cells), jnp.float32)
    for order in range(orders):
        product = jnp.dot(
            matrices[order],
            incoming,
            precision=lax.Precision.HIGHEST,
            preferred_element_type=jnp.float32,
        )
        total = total + kernel[order] * product
    return total.reshape(state.shape)


def per_device(
    state, coupling, fetch_group, live_slots, radius_one, radius_two, kinetic_diag, kinetic_link
):
    coupled = coupling_products(state, coupling, fetch_group, live_slots, radius_one, radius_two)
    state_here, coupled_here = (
        lax.all_to_all(state, "rad", split_axis=0, concat_axis=3, tiled=True),
        lax.all_to_all(coupled, "rad", split_axis=0, concat_axis=3, tiled=True),
    )
    applied = kinetic(state_here, kinetic_diag, kinetic_link) + coupled_here
    wave_re = applied[:, 1]
    wave_im = -applied[:, 0]
    state_re = state_here[:, 0]
    state_im = state_here[:, 1]
    total_count = 2.0 * C * state.shape[2] * R
    cross_re = jnp.sum(state_re * wave_re + state_im * wave_im)
    cross_im = jnp.sum(state_re * wave_im - state_im * wave_re)
    self_sq = jnp.sum(state_here * state_here)
    cross_re, cross_im, self_sq = lax.psum((cross_re, cross_im, self_sq), ("chan", "rad"))
    proj_re = cross_re / self_sq
    proj_im = cross_im / self_sq
    orth_re = wave_re - (proj_re * state_re - proj_im * state_im)
    orth_im = wave_im - (proj_re * state_im + proj_im * state_re)
    square_mean = (
        lax.psum(jnp.sum(orth_re * orth_re + orth_im * orth_im), ("chan", "rad")) / total_count
    )
    rms = jnp.sqrt(square_mean + 1e-06)
    orthogonal = jnp.stack([orth_re, orth_im], axis=1)
    return (orthogonal, jnp.stack([proj_re, proj_im, rms]))


def solution(mesh):
    placed = (
        P("chan", None, None, "rad"),
        P("chan", None, None, None, None),
        P(),
        P("chan"),
        P(),
        P("rad"),
        P(),
        P(),
    )
    return jax.shard_map(
        per_device,
        mesh=mesh,
        in_specs=placed,
        out_specs=(P(("chan", "rad"), None, None, None), P()),
        check_vma=False,
    )
```

profile of v0, /device:TPU:1, one launch (start us, length us, event | category | flops | bytes accessed | tf_op | source)
XLA Modules:
  0.0 410.5 jit_solution(6286049403578286027)
XLA Ops:
  2.5 3.0 copy.55
  5.5 2.5 reshape.226
  8.0 3.6 gather_fusion.1
  11.7 6.5 %broadcast_select_fusion = f32[16,32,3072]{2,1,0:T(8,128)} fusion(f32[16,32,3072]{2,1,0:T(8,128)} %gather_fusion.1, pred[16]{0:T(512)(128)(4,1)S(1)} %and_reduce_fusion), kind=kLoop, calls=%fused_computation.11 | loop fusion | flops 1572864 | bytes 12582928 | tf_op jit(solution)/shard_map/jit(_take)/select_n | solution.py:42
  18.1 10.0 %all-to-all-start.1 = ((f32[16,32,3072]{2,1,0:T(8,128)}), f32[16,32,3072]{2,1,0:T(8,128)}, u32[]{:S(2)}, u32[]{:S(2)}) async-start(f32[16,32,3072]{2,1,0:T(8,128)} %broadcast_select_fusion), calls=%async_computation.1 | async-start | bytes 12582912 | tf_op jit(solution)/shard_map/all_to_all | solution.py:43
  28.2 5.0 %gather_fusion = f32[16,4,4,32,32]{4,3,2,1,0:T(8,128)} fusion(f32[4,16,4,32,32]{4,3,2,1,0:T(8,128)} %param.9, s32[1024]{0:T(1024)S(1)} %pad_clamp_fusion.1), kind=kCustom, calls=%fused_computation | custom fusion | bytes 2097216 | tf_op jit(solution)/shard_map/jit(_take)/gather | solution.py:46
  33.3 2.5 fusion
  35.9 1.9 fusion.24
  46.3 120.3 %all-to-all-done.1 = f32[16,32,3072]{2,1,0:T(8,128)} async-done(((f32[16,32,3072]{2,1,0:T(8,128)}), f32[16,32,3072]{2,1,0:T(8,128)}, u32[]{:S(2)}, u32[]{:S(2)}) %all-to-all-start.1) | async-done | bytes 6291488 | tf_op jit(solution)/shard_map/all_to_all | solution.py:43
  166.6 6.8 %all-to-all-start = ((f32[128,2,16,96]{3,2,1,0:T(8,128)}), f32[128,2,16,96]{3,2,1,0:T(8,128)S(1)}, u32[]{:S(2)}, u32[]{:S(2)}) async-start(f32[128,2,16,96]{3,2,1,0:T(8,128)} %copy.55), calls=%async_computation | async-start | bytes 4194304 | tf_op jit(solution)/shard_map/all_to_all | solution.py:71
  173.4 5.6 %convolution_multiply_fusion.3 = f32[128,3072]{1,0:T(8,128)S(1)} fusion(f32[128,512]{1,0:T(8,128)S(1)} %squeeze.23, f32[512,3072]{1,0:T(8,128)} %bitcast.8, f32[3072]{0:T(1024)S(1)} %broadcast_in_dim.51), kind=kOutput, calls=%fused_computation.10 | convolution fusion | flops 2416312320 | bytes 8138752 | tf_op jit(solution)/shard_map/dot_general | solution.py:56
  179.0 5.6 %fusion.3 = f32[128,3072]{1,0:T(8,128)S(1)} fusion(f32[128,3072]{1,0:T(8,128)S(1)} %convolution_multiply_fusion.3, f32[128,512]{1,0:T(8,128)S(1)} %squeeze.24, f32[512,3072]{1,0:T(8,128)} %bitcast.8, f32[3072]{0:T(1024)S(1)} %broadcast_in_dim.57), kind=kOutput, calls=%fused_computation.9 | convolution fusion | flops 2416705536 | bytes 9711616 | tf_op jit(solution)/shard_map/dot_general | solution.py:56
  184.6 5.6 %fusion.2 = f32[128,3072]{1,0:T(8,128)S(1)} fusion(f32[128,3072]{1,0:T(8,128)S(1)} %fusion.3, f32[128,512]{1,0:T(8,128)S(1)} %copy-done.6, f32[512,3072]{1,0:T(8,128)} %bitcast.8, f32[3072]{0:T(1024)S(1)} %broadcast_in_dim.59), kind=kOutput, calls=%fused_computation.7 | convolution fusion | flops 2416705536 | bytes 9711616 | tf_op jit(solution)/shard_map/dot_general | solution.py:56
  190.2 7.3 %fusion.1 = f32[128,3072]{1,0:T(8,128)} fusion(f32[128,3072]{1,0:T(8,128)S(1)} %fusion.2, f32[128,512]{1,0:T(8,128)S(1)} %copy-done.7, f32[512,3072]{1,0:T(8,128)} %bitcast.8, f32[3072]{0:T(1024)S(1)} %broadcast_in_dim.61), kind=kOutput, calls=%fused_computation.5 | convolution fusion | flops 2416705536 | bytes 9711616 | tf_op jit(solution)/shard_map/dot_general | solution.py:56
  197.6 3.0 copy.67
  200.6 3.0 copy.68
  204.9 6.7 %all-to-all-start.2 = ((f32[128,2,16,96]{3,2,1,0:T(8,128)}), f32[128,2,16,96]{3,2,1,0:T(8,128)}, u32[]{:S(2)}, u32[]{:S(2)}) async-start(f32[128,2,16,96]{3,2,1,0:T(8,128)} %copy.68), calls=%async_computation.2 | async-start | bytes 4194304 | tf_op jit(solution)/shard_map/all_to_all | solution.py:72
  211.7 2.8 copy.56
  217.5 2.2 all_to_all.37
  219.7 2.2 copy.57
  224.8 2.8 fusion.4
  227.6 2.9 copy.61
  230.5 2.6 reshape.225
  233.1 2.7 multiply_reduce_fusion
  235.8 4.0 all-to-all-done.2
  239.8 4.1 %copy.69 = f32[8,2,16,16,96]{4,3,2,1,0:T(8,128)} copy(f32[8,2,16,16,96]{4,2,1,0,3:T(8,128)} %bitcast.14) | data formatting | bytes 3145728 | tf_op jit(solution)/shard_map/all_to_all | solution.py:72
  244.0 3.1 all_to_all.36
  247.0 2.1 add.110
  250.3 77.7 %all-reduce.2 = (f32[]{:T(128)}, f32[]{:T(128)}, f32[]{:T(128)}) all-reduce(f32[]{:T(128)} %get-tuple-element.3, f32[]{:T(128)} %multiply_reduce_fusion, f32[]{:T(128)} %get-tuple-element.2), channel_id=1, replica_groups=mesh['chan'=16,'rad'=16] {'chan','rad'}, use_global_device_ids=true, to_apply=%region_5.6 | all-reduce | flops 3 | bytes 24 | tf_op jit(solution)/shard_map/psum | solution.py:83
  330.5 2.4 fusion.13
  334.2 72.6 %psum.31 = f32[]{:T(128)} all-reduce(f32[]{:T(128)} %fusion.13), channel_id=1, replica_groups=mesh['chan'=16,'rad'=16] {'chan','rad'}, use_global_device_ids=true, to_apply=%region_7.8 | all-reduce | flops 1 | bytes 8 | tf_op jit(solution)/shard_map/psum | solution.py:89
  407.5 2.4 pad_maximum_fusion
  (58 shorter events, 20.7 us)
Async XLA Ops:
  0.6 224.2 %copy-start = (f32[12,128,128]{2,1,0:T(8,128)S(1)}, f32[12,128,128]{2,1,0:T(8,128)}, u32[]{:S(2)}) copy-start(f32[12,128,128]{2,1,0:T(8,128)} %param.14) | copy-start | bytes 2359300
  18.1 148.5 %all-to-all-start.1 = ((f32[16,32,3072]{2,1,0:T(8,128)}), f32[16,32,3072]{2,1,0:T(8,128)}, u32[]{:S(2)}, u32[]{:S(2)}) async-start(f32[16,32,3072]{2,1,0:T(8,128)} %broadcast_select_fusion), calls=%async_computation.1 | async-start | bytes 12582912 | tf_op jit(solution)/shard_map/all_to_all | solution.py:43
  28.2 5.0 %copy-start.8 = (s32[4]{0:T(128)S(1)}, s32[4]{0:T(128)}, u32[]{:S(2)}) copy-start(s32[4]{0:T(128)} %param.11) | copy-start | bytes 52
  37.8 1.1 copy-start.9
  37.8 1.1 copy-start.10
  166.6 37.0 %all-to-all-start = ((f32[128,2,16,96]{3,2,1,0:T(8,128)}), f32[128,2,16,96]{3,2,1,0:T(8,128)S(1)}, u32[]{:S(2)}, u32[]{:S(2)}) async-start(f32[128,2,16,96]{3,2,1,0:T(8,128)} %copy.55), calls=%async_computation | async-start | bytes 4194304 | tf_op jit(solution)/shard_map/all_to_all | solution.py:71
  179.0 5.6 %copy-start.6 = (f32[128,512]{1,0:T(8,128)S(1)}, f32[128,512]{1,0:T(8,128)}, u32[]{:S(2)}) copy-start(f32[128,512]{1,0:T(8,128)} %squeeze.25) | copy-start | bytes 786436
  184.6 5.6 %copy-start.7 = (f32[128,512]{1,0:T(8,128)S(1)}, f32[128,512]{1,0:T(8,128)}, u32[]{:S(2)}) copy-start(f32[128,512]{1,0:T(8,128)} %squeeze.26) | copy-start | bytes 786436
  203.6 1.3 copy-start.4
  204.9 34.9 %all-to-all-start.2 = ((f32[128,2,16,96]{3,2,1,0:T(8,128)}), f32[128,2,16,96]{3,2,1,0:T(8,128)}, u32[]{:S(2)}, u32[]{:S(2)}) async-start(f32[128,2,16,96]{3,2,1,0:T(8,128)} %copy.68), calls=%async_computation.2 | async-start | bytes 4194304 | tf_op jit(solution)/shard_map/all_to_all | solution.py:72
  214.4 1.4 copy-start.3
  219.7 2.2 copy-start.5
  249.1 1.1 copy-start.1
  330.5 2.4 copy-start.2
where the time goes:
time: 412 us; the launch traced here: 410 us
  blocking collectives  150 us (36%)
  waiting for transfers between devices  124 us (30%)
  local copies, waits for them, and re-layouts  54.6 us (13%)
  matrix products  29.7 us (7%)
  other arithmetic  23.9 us (6%)
  starting transfers between devices  23.5 us (6%)
  between operations  4.18 us (1%)
    all_to_all x1, waiting for transfers between devices, coupling_products(): lax.all_to_all(outgoing, 'chan', split_axis=0, concat_axis=0, tiled=True)  120 us
    psum x1, blocking collectives, per_device(): lax.psum((cross_re, cross_im, self_sq), ('chan', 'rad'))  77.7 us
    psum x1, blocking collectives, per_device(): lax.psum(jnp.sum(orth_re * orth_re + orth_im * orth_im), ('chan', 'rad'))  72.6 us
    dot_general x4, matrix products, coupling_products(): jnp.dot(matrices[order], incoming, precision=lax.Precision.HIGHEST, prefe...  24.1 us
    all_to_all x1, starting transfers between devices, coupling_products(): lax.all_to_all(outgoing, 'chan', split_axis=0, concat_axis=0, tiled=True)  9.98 us
  transfers between devices with their start and end apart: 3, of which 2 were waited for; matrix products, arithmetic and copies ran while one was open for 17% of the time, Pallas kernels for 0%

commit v1 on v0

--- a/solution.py
+++ b/solution.py
@@ -2,6 +2,7 @@
 import jax.numpy as jnp
 from jax import lax
 from jax.sharding import PartitionSpec as P
+from jax.lax import psum
 
 C = 2048
 R = 1536
@@ -80,7 +81,10 @@
     cross_re = jnp.sum(state_re * wave_re + state_im * wave_im)
     cross_im = jnp.sum(state_re * wave_im - state_im * wave_re)
     self_sq = jnp.sum(state_here * state_here)
-    cross_re, cross_im, self_sq = lax.psum((cross_re, cross_im, self_sq), ("chan", "rad"))
+    obtain_tables = lambda incoming_x, net_axis, a_name: psum(
+        psum(incoming_x, axis_name=a_name), axis_name=net_axis
+    )
+    cross_re, cross_im, self_sq = obtain_tables((cross_re, cross_im, self_sq), "rad", "chan")
     proj_re = cross_re / self_sq
     proj_im = cross_im / self_sq
     orth_re = wave_re - (proj_re * state_re - proj_im * state_im)

time: 412 us -> 398 us (0.966)
  blocking collectives: 150 us -> 136 us
    psum x1 -> x2, blocking collectives: 77.7 us -> 56.8 us  [the longest x1 29.6 us: per_device(): psum(psum(incoming_x, axis_name=a_name), axis_name=net_axis)]
    psum x1, blocking collectives: 72.6 us -> 79.7 us  [per_device(): lax.psum(jnp.sum(orth_re * orth_re + orth_im * orth_im), ('chan', 'rad'))]
where the time goes in v1:
time: 398 us; the launch traced here: 397 us
  blocking collectives  136 us (34%)
  waiting for transfers between devices  124 us (31%)
  local copies, waits for them, and re-layouts  54.6 us (14%)
  matrix products  29.7 us (7%)
  other arithmetic  23.9 us (6%)
  starting transfers between devices  23.5 us (6%)
  between operations  4.17 us (1%)
    all_to_all x1, waiting for transfers between devices, coupling_products(): lax.all_to_all(outgoing, 'chan', split_axis=0, concat_axis=0, tiled=True)  120 us
    psum x1, blocking collectives, per_device(): lax.psum(jnp.sum(orth_re * orth_re + orth_im * orth_im), ('chan', 'rad'))  79.7 us
    psum x1, blocking collectives, per_device(): psum(psum(incoming_x, axis_name=a_name), axis_name=net_axis)  29.6 us
    psum x1, blocking collectives, per_device(): psum(incoming_x, axis_name=a_name)  27.2 us
    dot_general x4, matrix products, coupling_products(): jnp.dot(matrices[order], incoming, precision=lax.Precision.HIGHEST, prefe...  24.1 us
    all_to_all x1, starting transfers between devices, coupling_products(): lax.all_to_all(outgoing, 'chan', split_axis=0, concat_axis=0, tiled=True)  9.98 us
  transfers between devices with their start and end apart: 3, of which 2 were waited for; matrix products, arithmetic and copies ran while one was open for 17% of the time, Pallas kernels for 0%

profile of v1, /device:TPU:1, one launch (start us, length us, event | category | flops | bytes accessed | tf_op | source)
XLA Modules:
  0.0 396.6 jit_solution(2488913897957221060)
XLA Ops:
  2.5 3.0 copy.55
  5.5 2.5 reshape.226
  8.0 3.6 gather_fusion.1
  11.7 6.5 %broadcast_select_fusion = f32[16,32,3072]{2,1,0:T(8,128)} fusion(f32[16,32,3072]{2,1,0:T(8,128)} %gather_fusion.1, pred[16]{0:T(512)(128)(4,1)S(1)} %and_reduce_fusion), kind=kLoop, calls=%fused_computation.11 | loop fusion | flops 1572864 | bytes 12582928 | tf_op jit(solution)/shard_map/jit(_take)/select_n | solution.py:43
  18.1 10.0 %all-to-all-start.1 = ((f32[16,32,3072]{2,1,0:T(8,128)}), f32[16,32,3072]{2,1,0:T(8,128)}, u32[]{:S(2)}, u32[]{:S(2)}) async-start(f32[16,32,3072]{2,1,0:T(8,128)} %broadcast_select_fusion), calls=%async_computation.1 | async-start | bytes 12582912 | tf_op jit(solution)/shard_map/all_to_all | solution.py:44
  28.2 5.0 %gather_fusion = f32[16,4,4,32,32]{4,3,2,1,0:T(8,128)} fusion(f32[4,16,4,32,32]{4,3,2,1,0:T(8,128)} %param.9, s32[1024]{0:T(1024)S(1)} %pad_clamp_fusion.1), kind=kCustom, calls=%fused_computation | custom fusion | bytes 2097216 | tf_op jit(solution)/shard_map/jit(_take)/gather | solution.py:47
  33.3 2.5 fusion
  46.3 120.3 %all-to-all-done.1 = f32[16,32,3072]{2,1,0:T(8,128)} async-done(((f32[16,32,3072]{2,1,0:T(8,128)}), f32[16,32,3072]{2,1,0:T(8,128)}, u32[]{:S(2)}, u32[]{:S(2)}) %all-to-all-start.1) | async-done | bytes 6291488 | tf_op jit(solution)/shard_map/all_to_all | solution.py:44
  166.6 6.8 %all-to-all-start = ((f32[128,2,16,96]{3,2,1,0:T(8,128)}), f32[128,2,16,96]{3,2,1,0:T(8,128)S(1)}, u32[]{:S(2)}, u32[]{:S(2)}) async-start(f32[128,2,16,96]{3,2,1,0:T(8,128)} %copy.55), calls=%async_computation | async-start | bytes 4194304 | tf_op jit(solution)/shard_map/all_to_all | solution.py:72
  173.4 5.6 %convolution_multiply_fusion.3 = f32[128,3072]{1,0:T(8,128)S(1)} fusion(f32[128,512]{1,0:T(8,128)S(1)} %squeeze.23, f32[512,3072]{1,0:T(8,128)} %bitcast.8, f32[3072]{0:T(1024)S(1)} %broadcast_in_dim.51), kind=kOutput, calls=%fused_computation.10 | convolution fusion | flops 2416312320 | bytes 8138752 | tf_op jit(solution)/shard_map/dot_general | solution.py:57
  179.0 5.6 %fusion.3 = f32[128,3072]{1,0:T(8,128)S(1)} fusion(f32[128,3072]{1,0:T(8,128)S(1)} %convolution_multiply_fusion.3, f32[128,512]{1,0:T(8,128)S(1)} %squeeze.24, f32[512,3072]{1,0:T(8,128)} %bitcast.8, f32[3072]{0:T(1024)S(1)} %broadcast_in_dim.57), kind=kOutput, calls=%fused_computation.9 | convolution fusion | flops 2416705536 | bytes 9711616 | tf_op jit(solution)/shard_map/dot_general | solution.py:57
  184.6 5.6 %fusion.2 = f32[128,3072]{1,0:T(8,128)S(1)} fusion(f32[128,3072]{1,0:T(8,128)S(1)} %fusion.3, f32[128,512]{1,0:T(8,128)S(1)} %copy-done.6, f32[512,3072]{1,0:T(8,128)} %bitcast.8, f32[3072]{0:T(1024)S(1)} %broadcast_in_dim.59), kind=kOutput, calls=%fused_computation.7 | convolution fusion | flops 2416705536 | bytes 9711616 | tf_op jit(solution)/shard_map/dot_general | solution.py:57
  190.2 7.3 %fusion.1 = f32[128,3072]{1,0:T(8,128)} fusion(f32[128,3072]{1,0:T(8,128)S(1)} %fusion.2, f32[128,512]{1,0:T(8,128)S(1)} %copy-done.7, f32[512,3072]{1,0:T(8,128)} %bitcast.8, f32[3072]{0:T(1024)S(1)} %broadcast_in_dim.61), kind=kOutput, calls=%fused_computation.5 | convolution fusion | flops 2416705536 | bytes 9711616 | tf_op jit(solution)/shard_map/dot_general | solution.py:57
  197.6 3.0 copy.67
  200.6 3.0 copy.68
  204.9 6.7 %all-to-all-start.2 = ((f32[128,2,16,96]{3,2,1,0:T(8,128)}), f32[128,2,16,96]{3,2,1,0:T(8,128)}, u32[]{:S(2)}, u32[]{:S(2)}) async-start(f32[128,2,16,96]{3,2,1,0:T(8,128)} %copy.68), calls=%async_computation.2 | async-start | bytes 4194304 | tf_op jit(solution)/shard_map/all_to_all | solution.py:73
  211.7 2.8 copy.56
  217.5 2.2 all_to_all.37
  219.7 2.2 copy.57
  224.8 2.8 fusion.4
  227.6 2.9 copy.61
  230.5 2.6 reshape.225
  233.1 2.7 multiply_reduce_fusion
  235.8 4.0 %all-to-all-done.2 = f32[128,2,16,96]{3,2,1,0:T(8,128)} async-done(((f32[128,2,16,96]{3,2,1,0:T(8,128)}), f32[128,2,16,96]{3,2,1,0:T(8,128)}, u32[]{:S(2)}, u32[]{:S(2)}) %all-to-all-start.2) | async-done | bytes 1572896 | tf_op jit(solution)/shard_map/all_to_all | solution.py:73
  239.8 4.1 %copy.69 = f32[8,2,16,16,96]{4,3,2,1,0:T(8,128)} copy(f32[8,2,16,16,96]{4,2,1,0,3:T(8,128)} %bitcast.14) | data formatting | bytes 3145728 | tf_op jit(solution)/shard_map/all_to_all | solution.py:73
  244.0 3.1 all_to_all.36
  247.0 2.1 add.116
  250.3 27.2 %all-reduce.3 = (f32[]{:T(128)}, f32[]{:T(128)}, f32[]{:T(128)}) all-reduce(f32[]{:T(128)} %get-tuple-element.3, f32[]{:T(128)} %multiply_reduce_fusion, f32[]{:T(128)} %get-tuple-element.2), channel_id=1, replica_groups=mesh['chan'=16,'rad'=16] {'chan'}, use_global_device_ids=true, to_apply=%region_7.8 | all-reduce | flops 3 | bytes 24 | tf_op jit(solution)/shard_map/psum | solution.py:85
  277.5 29.6 %all-reduce.2 = (f32[]{:T(128)}, f32[]{:T(128)}, f32[]{:T(128)}) all-reduce(f32[]{:T(128)} %get-tuple-element.7, f32[]{:T(128)} %get-tuple-element.8, f32[]{:T(128)} %get-tuple-element.9), channel_id=1, replica_groups=mesh['chan'=16,'rad'=16] {'rad'}, use_global_device_ids=true, to_apply=%region_8.9 | all-reduce | flops 3 | bytes 24 | tf_op jit(solution)/shard_map/psum | solution.py:84
  309.6 2.4 fusion.13
  313.2 79.7 %psum.55 = f32[]{:T(128)} all-reduce(f32[]{:T(128)} %fusion.13), channel_id=1, replica_groups=mesh['chan'=16,'rad'=16] {'chan','rad'}, use_global_device_ids=true, to_apply=%region_10.11 | all-reduce | flops 1 | bytes 8 | tf_op jit(solution)/shard_map/psum | solution.py:93
  393.6 2.4 pad_maximum_fusion
  (59 shorter events, 22.6 us)
Async XLA Ops:
  0.6 224.2 %copy-start = (f32[12,128,128]{2,1,0:T(8,128)S(1)}, f32[12,128,128]{2,1,0:T(8,128)}, u32[]{:S(2)}) copy-start(f32[12,128,128]{2,1,0:T(8,128)} %param.14) | copy-start | bytes 2359300
  18.1 148.5 %all-to-all-start.1 = ((f32[16,32,3072]{2,1,0:T(8,128)}), f32[16,32,3072]{2,1,0:T(8,128)}, u32[]{:S(2)}, u32[]{:S(2)}) async-start(f32[16,32,3072]{2,1,0:T(8,128)} %broadcast_select_fusion), calls=%async_computation.1 | async-start | bytes 12582912 | tf_op jit(solution)/shard_map/all_to_all | solution.py:44
  28.2 5.0 %copy-start.8 = (s32[4]{0:T(128)S(1)}, s32[4]{0:T(128)}, u32[]{:S(2)}) copy-start(s32[4]{0:T(128)} %param.11) | copy-start | bytes 52
  37.8 1.1 copy-start.9
  37.8 1.1 copy-start.10
  166.6 37.0 %all-to-all-start = ((f32[128,2,16,96]{3,2,1,0:T(8,128)}), f32[128,2,16,96]{3,2,1,0:T(8,128)S(1)}, u32[]{:S(2)}, u32[]{:S(2)}) async-start(f32[128,2,16,96]{3,2,1,0:T(8,128)} %copy.55), calls=%async_computation | async-start | bytes 4194304 | tf_op jit(solution)/shard_map/all_to_all | solution.py:72
  179.0 5.6 %copy-start.6 = (f32[128,512]{1,0:T(8,128)S(1)}, f32[128,512]{1,0:T(8,128)}, u32[]{:S(2)}) copy-start(f32[128,512]{1,0:T(8,128)} %squeeze.25) | copy-start | bytes 786436
  184.6 5.6 %copy-start.7 = (f32[128,512]{1,0:T(8,128)S(1)}, f32[128,512]{1,0:T(8,128)}, u32[]{:S(2)}) copy-start(f32[128,512]{1,0:T(8,128)} %squeeze.26) | copy-start | bytes 786436
  203.6 1.3 copy-start.4
  204.9 34.9 %all-to-all-start.2 = ((f32[128,2,16,96]{3,2,1,0:T(8,128)}), f32[128,2,16,96]{3,2,1,0:T(8,128)}, u32[]{:S(2)}, u32[]{:S(2)}) async-start(f32[128,2,16,96]{3,2,1,0:T(8,128)} %copy.68), calls=%async_computation.2 | async-start | bytes 4194304 | tf_op jit(solution)/shard_map/all_to_all | solution.py:73
  214.4 1.4 copy-start.3
  219.7 2.2 copy-start.5
  249.1 1.1 copy-start.1
  309.6 2.4 copy-start.2
